TPU v7x, 256 devices: a whole 4x4x8 slice. The times are simulated.
256 devices in a mesh: rows: 32 (over x, z_hi, core), mask: 8 (over z_lo, y).
Axes of the slice: x: 4, y: 4, z: 8 (z_hi: 4, z_lo: 2; z = z_hi * 2 + z_lo), core: 2. Of those that a mesh axis runs over, the one named last changes fastest.
Arguments:
- image_field: bfloat16 [2, 8192, 8192], P(None, ('rows', 'mask')), may hold values from -6 to 6
- amplitudes: bfloat16 [8, 8192, 8192], P('mask', None, 'rows'), may hold values from 0 to 12, as said below
- mask_ids: int32 [8], P('mask'), may hold values from 0 to 63
Outputs:
- gradient: float32 [2, 8192, 8192], P(None, ('rows', 'mask'))
- loss_value: float32 [], replicated
Inputs may be any that keep to these rules, and one draw needn't show every extreme that they name: `amplitudes`: magnitudes are non-negative.
All inputs are finite; a program needn't handle non-finite values.
Results may differ from a plain program's by a relative error of at most 0.024.
Values may be sent and summed in bfloat16 or wider, within the bound.
A program may use at most 128 MiB of HBM per device.

v0:
```python
import math
import jax
import jax.numpy as jnp
from jax import lax
from jax.sharding import PartitionSpec as P

INNER = 128
EPSILON = 0.25


def shift_bits(values, count):
    return lax.shift_right_logical(values, jnp.full(values.shape, count, jnp.int32))


def mask_code(window_id, row_index, column_index):
    mixed = (
        row_index * jnp.int32(73856093)
        ^ column_index * jnp.int32(19349663)
        ^ (window_id + jnp.int32(1)) * jnp.int32(83492791)
    )
    mixed = mixed ^ shift_bits(mixed, 13)
    mixed = mixed * jnp.int32(1274126177)
    mixed = mixed ^ shift_bits(mixed, 16)
    return shift_bits(mixed, 28) & jnp.int32(3)


def rotate(real_part, imag_part, phase_code, direction):
    cosine = (phase_code == 0).astype(jnp.float32) - (phase_code == 2).astype(jnp.float32)
    sine = direction * (
        (phase_code == 1).astype(jnp.float32) - (phase_code == 3).astype(jnp.float32)
    )
    return (real_part * cosine - imag_part * sine, real_part * sine + imag_part * cosine)


def factor_table(length, direction):
    index = jnp.arange(length, dtype=jnp.int32)
    angles = (index[:, None] * index[None, :] % length).astype(jnp.float32) * (
        2.0 * math.pi / length
    )
    cosine = jnp.cos(angles)
    sine = direction * jnp.sin(angles)
    upper = jnp.stack([cosine, -sine], axis=1)
    lower = jnp.stack([sine, cosine], axis=1)
    return jnp.stack([upper, lower]).astype(jnp.bfloat16)


def turn_table(outer, inner, length, direction):
    first = jnp.arange(outer, dtype=jnp.int32)[:, None]
    second = jnp.arange(inner, dtype=jnp.int32)[None, :]
    angles = (first * second % length).astype(jnp.float32) * (2.0 * math.pi / length)
    return (jnp.cos(angles), direction * jnp.sin(angles))


def factor(form, table, values):
    return jnp.einsum(form, table, values, preferred_element_type=jnp.float32)


def twist(real_part, imag_part, cosine, sine, axis):
    return jnp.stack(
        [real_part * cosine - imag_part * sine, real_part * sine + imag_part * cosine], axis=axis
    ).astype(jnp.bfloat16)


def rows_forward(values, tables):
    lead_table, sub_table, cosine, sine = tables
    batch, parts, count, length = values.shape
    view = values.reshape(batch, parts, count, lead_table.shape[1], sub_table.shape[1])
    first = factor("pkqj,xqrjb->xprkb", lead_table, view)
    middle = twist(first[:, 0], first[:, 1], cosine, sine, 1)
    second = factor("pkqj,xqraj->xprak", sub_table, middle)
    return second.reshape(batch, parts, count, length) * (1.0 / math.sqrt(length))


def rows_inverse(values, tables):
    lead_table, sub_table, cosine, sine = tables
    batch, parts, count, length = values.shape
    view = values.reshape(batch, parts, count, lead_table.shape[1], sub_table.shape[1])
    first = factor("pkqj,xqraj->xprak", sub_table, view)
    middle = twist(first[:, 0], first[:, 1], cosine, sine, 1)
    second = factor("pkqj,xqrjb->xprkb", lead_table, middle)
    return second.reshape(batch, parts, count, length) * (1.0 / math.sqrt(length))


def cols_forward(values, tables):
    lead_table, sub_table, cosine, sine = tables
    parts, length, width = values.shape
    view = values.reshape(parts, lead_table.shape[1], sub_table.shape[1], width)
    first = factor("pkqj,qjbw->pkbw", lead_table, view)
    middle = twist(first[0], first[1], cosine[:, :, None], sine[:, :, None], 0)
    second = factor("pkqj,qajw->pakw", sub_table, middle)
    return second.reshape(parts, length, width) * (1.0 / math.sqrt(length))


def cols_inverse(values, tables):
    lead_table, sub_table, cosine, sine = tables
    parts, length, width = values.shape
    view = values.reshape(parts, lead_table.shape[1], sub_table.shape[1], width)
    first = factor("pkqj,qajw->pakw", sub_table, view)
    middle = twist(first[0], first[1], cosine[:, :, None], sine[:, :, None], 0)
    second = factor("pkqj,qjbw->pkbw", lead_table, middle)
    return second.reshape(parts, length, width) * (1.0 / math.sqrt(length))


def shards(image_field, amplitudes, mask_ids):
    slab = lax.all_gather(image_field, "mask", axis=1, tiled=True)
    slab_rows = slab.shape[1]
    width = slab.shape[2]
    outer = width // INNER
    forward_cos, forward_sin = turn_table(outer, INNER, width, -1.0)
    inverse_cos, inverse_sin = turn_table(outer, INNER, width, 1.0)
    forward_tables = (
        factor_table(outer, -1.0),
        factor_table(INNER, -1.0),
        forward_cos,
        forward_sin,
    )
    inverse_tables = (factor_table(outer, 1.0), factor_table(INNER, 1.0), inverse_cos, inverse_sin)
    first_row = lax.axis_index("rows") * slab_rows
    row_index = first_row + jnp.arange(slab_rows, dtype=jnp.int32)[:, None]
    column_index = jnp.arange(width, dtype=jnp.int32)[None, :]
    phase_code = mask_code(mask_ids[0], row_index, column_index)
    masked_real, masked_imag = rotate(
        slab[0].astype(jnp.float32), slab[1].astype(jnp.float32), phase_code, 1.0
    )
    masked = jnp.stack([masked_real, masked_imag]).astype(jnp.bfloat16)
    outgoing = rows_forward(masked[None], forward_tables)[0].astype(jnp.bfloat16)
    column_slab = lax.all_to_all(outgoing, "rows", split_axis=2, concat_axis=1, tiled=True)
    spectrum = cols_forward(column_slab, forward_tables)
    spec_real = spectrum[0]
    spec_imag = spectrum[1]
    measured = amplitudes[0].astype(jnp.float32)
    magnitude = jnp.sqrt(spec_real * spec_real + spec_imag * spec_imag + EPSILON)
    factor_kept = 1.0 - measured / magnitude
    misfit = magnitude - measured
    loss_part = jnp.sum(misfit * misfit)
    weighted = jnp.stack([spec_real * factor_kept, spec_imag * factor_kept]).astype(jnp.bfloat16)
    returning = cols_inverse(weighted, inverse_tables).astype(jnp.bfloat16)
    row_slab = lax.all_to_all(returning, "rows", split_axis=1, concat_axis=2, tiled=True)
    back = rows_inverse(row_slab[None], inverse_tables)[0]
    term_real, term_imag = rotate(back[0], back[1], phase_code, -1.0)
    gradient = lax.psum_scatter(
        jnp.stack([term_real, term_imag]).astype(jnp.bfloat16),
        "mask",
        scatter_dimension=1,
        tiled=True,
    ).astype(jnp.float32)
    loss_total = lax.psum(loss_part, ("rows", "mask"))
    loss_value = loss_total / (lax.axis_size("mask") * width * width)
    return (gradient, loss_value)


def solution(mesh):
    return jax.shard_map(
        shards,
        mesh=mesh,
        in_specs=(P(None, ("rows", "mask"), None), P("mask", None, "rows"), P("mask")),
        out_specs=(P(None, ("rows", "mask"), None), P()),
        check_vma=False,
    )
```

profile of v0, /device:TPU:1, one launch (start us, length us, event | category | flops | bytes accessed | tf_op | source)
XLA Modules:
  0.0 996.1 jit_solution(3554799397838370587)
XLA Ops:
  7.2 0.7 all-gather.2.cloned.1.call-update
  8.7 0.1 cosine_convert_fusion.1
  9.0 0.3 fusion.77
  9.5 0.3 cosine_convert_fusion
  9.7 0.3 negate_convert_fusion
  10.1 98.1 %all-gather.2.cloned.1.call-done = bf16[2,256,8192]{2,1,0:T(8,128)(2,1)} async-done(((bf16[2,32,8192]{2,1,0:T(8,128)(2,1)}), bf16[2,256,8192]{2,1,0:T(8,128)(2,1)}) %all-gather.2.cloned.1.call-update) | async-done | bytes 8388624 | tf_op jit(solution)/shard_map/all_gather | solution.py:105
  108.2 9.7 fusion.49
  117.9 1.2 copy.123
  119.1 3.2 copy.122
  122.3 4.6 convolution_bitcast_fusion
  126.8 2.3 fusion.47
  129.2 3.8 fusion.46
  133.0 6.2 maximum_bitcast_fusion.2
  139.2 16.8 %fusion.41 = bf16[1,2,256,64,128]{2,4,1,3,0:T(8,128)(2,1)} fusion(bf16[2,256,64,128,1]{3,2,1,0,4:T(8,128)(2,1)} %maximum_bitcast_fusion.2, bf16[1,128,2,128]{3,1,2,0:T(8,128)(2,1)S(1)} %get-tuple-element.21, bf16[1,128,2,128]{3,1,2,0:T(8,128)(2,1)S(1)} %get-tuple-element.22), kind=kOutput, calls=%fused_computation.77 | convolution fusion | flops 2156134400 | bytes 16908288 | tf_op jit(solution)/shard_map/pkqj,xqraj->xprak/dot_general | solution.py:55
  156.0 7.7 copy.71
  163.7 16.4 %copy.72 = bf16[2,256,8192]{1,0,2:T(2,128)(2,1)} copy(bf16[2,256,8192]{1,2,0:T(8,128)(2,1)} %bitcast.205) | data formatting | bytes 16777216 | tf_op jit(solution)/shard_map/convert_element_type | solution.py:126
  180.1 9.4 all-to-all-start
  189.6 0.4 reduce-scatter.2.cloned.1.call-start
  190.5 148.9 %all-to-all-done = bf16[2,256,8192]{1,0,2:T(2,128)(2,1)} async-done(((bf16[2,256,8192]{1,0,2:T(2,128)(2,1)}), bf16[2,256,8192]{1,0,2:T(2,128)(2,1)}, u32[]{:S(2)}, u32[]{:S(2)}) %all-to-all-start) | async-done | bytes 8388640 | tf_op jit(solution)/shard_map/all_to_all | solution.py:127
  339.4 7.7 copy.73
  347.1 12.0 %copy.74 = bf16[2,32,256,256]{3,2,1,0:T(8,128)(2,1)} copy(bf16[2,32,256,256]{2,3,1,0:T(8,128)(2,1)} %bitcast.206) | data formatting | bytes 16777216 | tf_op jit(solution)/shard_map/all_to_all | solution.py:127
  359.1 9.7 fusion.36
  368.8 5.4 subtract_convert_fusion.3
  374.2 6.2 maximum_bitcast_fusion.3
  380.4 10.0 %fusion.2 = f32[2,64,128,256]{3,2,0,1:T(8,128)S(1)} fusion(bf16[2,64,128,256,1]{3,1,2,0,4:T(8,128)(2,1)} %maximum_bitcast_fusion.3, bf16[1,128,2,128]{3,1,2,0:T(8,128)(2,1)S(1)} %get-tuple-element.21, bf16[1,128,2,128]{3,1,2,0:T(8,128)(2,1)S(1)} %get-tuple-element.22), kind=kOutput, calls=%fused_computation.5 | convolution fusion | flops 2151940096 | bytes 25296896 | tf_op jit(solution)/shard_map/pkqj,qajw->pakw/dot_general | solution.py:55
  390.4 6.6 fusion.97
  397.0 12.9 %fusion.10 = (f32[]{:T(128)}, bf16[1,8192,256]{2,1,0:T(8,128)(2,1)}, bf16[1,8192,256]{2,1,0:T(8,128)(2,1)}) fusion(bf16[1,8192,256]{2,1,0:T(8,128)(2,1)S(1)} %copy-done, f32[1,8192,256]{2,1,0:T(8,128)} %bitcast.211, f32[1,8192,256]{2,1,0:T(8,128)} %bitcast.210), kind=kLoop, calls=%fused_computation.24 | loop fusion | flops 29360128 | bytes 29360132 | tf_op jit(solution)/shard_map/reduce_sum | solution.py:135
  409.8 6.4 copy.80
  416.2 6.4 copy.79
  422.7 11.6 %convolution_bitcast_fusion.1 = f32[64,256,2,128]{3,1,2,0:T(8,128)} fusion(bf16[1,64,128,256]{2,3,0,1:T(8,128)(2,1)} %copy.80, bf16[1,64,128,256]{2,3,0,1:T(8,128)(2,1)} %copy.79, bf16[1,128,2,128]{3,1,2,0:T(8,128)(2,1)S(1)} %get-tuple-element.20, bf16[1,128,2,128]{3,1,2,0:T(8,128)(2,1)S(1)} %get-tuple-element.19), kind=kOutput, calls=%fused_computation.17 | convolution fusion | flops 2164523008 | bytes 25296896 | tf_op jit(solution)/shard_map/pkqj,qajw->pakw/dot_general | solution.py:55
  434.2 17.4 %copy.81 = f32[64,256,2,128]{1,0,3,2:T(8,128)} copy(f32[64,256,2,128]{3,1,2,0:T(8,128)} %convolution_bitcast_fusion.1) | data formatting | bytes 33554432 | tf_op jit(solution)/shard_map/pkqj,qajw->pakw/dot_general | solution.py:55
  451.7 7.9 subtract_convert_fusion.2
  459.6 4.9 fusion.1
  464.5 11.4 %copy.84 = bf16[2,64,128,256]{3,2,1,0:T(8,128)(2,1)} copy(bf16[2,64,128,256]{3,1,2,0:T(8,128)(2,1)} %fusion.1) | data formatting | bytes 16777216 | tf_op jit(solution)/shard_map/convert_element_type | solution.py:137
  475.9 14.5 %copy.85 = bf16[2,8192,256]{2,0,1:T(2,128)(2,1)S(1)} copy(bf16[2,8192,256]{2,1,0:T(8,128)(2,1)} %bitcast.207) | data formatting | bytes 16777216 | tf_op jit(solution)/shard_map/convert_element_type | solution.py:137
  490.4 167.5 %all_to_all.30 = bf16[2,8192,256]{2,0,1:T(2,128)(2,1)} all-to-all(bf16[2,8192,256]{2,0,1:T(2,128)(2,1)S(1)} %copy.85), channel_id=1, replica_groups=mesh['rows'=32,'mask'=8] {'rows'}, dimensions={1} | all-to-all | bytes 16777216 | tf_op jit(solution)/shard_map/all_to_all | solution.py:138
  657.9 7.7 copy.86
  665.6 12.0 %copy.87 = bf16[2,256,32,256]{1,3,2,0:T(8,128)(2,1)} copy(bf16[2,256,32,256]{3,1,2,0:T(8,128)(2,1)} %bitcast.208) | data formatting | bytes 16777216 | tf_op jit(solution)/shard_map/all_to_all | solution.py:138
  677.6 12.0 %copy.105 = bf16[2,256,64,128,1]{3,2,0,1,4:T(8,128)(2,1)} copy(bf16[2,256,64,128,1]{1,3,2,0,4:T(8,128)(2,1)} %bitcast.209) | data formatting | bytes 16777216 | tf_op jit(solution)/shard_map/reshape.18
  689.6 5.5 convolution_bitcast_fusion.2
  695.1 2.5 fusion.44
  697.6 7.1 fusion
  704.7 20.0 %mul.910 = f32[1,2,256,8192]{3,1,2,0:T(2,128)} reshape(f32[1,2,256,64,128]{4,3,1,2,0:T(8,128)} %fusion) | data formatting | bytes 33554432 | tf_op jit(solution)/shard_map/mul | solution.py:81
  724.7 21.0 %fusion.96 = (f32[1,1,256,8192]{3,1,2,0:T(1,128)S(1)}, f32[1,1,256,8192]{3,1,2,0:T(1,128)}) fusion(f32[1,2,256,8192]{3,1,2,0:T(2,128)} %mul.910), kind=kLoop, calls=%fused_computation.162 | loop fusion | bytes 33554432 | tf_op jit(solution)/shard_map/slice | solution.py:140
  745.8 20.7 %subtract_convert_fusion = (bf16[1,256,8192]{2,1,0:T(8,128)(2,1)S(1)}, bf16[1,256,8192]{2,1,0:T(8,128)(2,1)}) fusion(f32[1,1,256,8192]{3,1,2,0:T(1,128)} %get-tuple-element.14, f32[1,1,256,8192]{3,1,2,0:T(1,128)S(1)} %get-tuple-element.13, s32[]{:T(128)} %bitcast.8, s32[8192]{0:T(1024)S(1)} %copy-done.2, s32[256]{0:T(256)S(1)} %copy-done.4), kind=kLoop, calls=%fused_computation.58 | loop fusion | flops 58720256 | bytes 25199620 | tf_op jit(solution)/shard_map/convert.1
  766.5 6.2 pad_maximum_fusion.1
  772.7 211.5 %psum.7 = f32[]{:T(128)} all-reduce(f32[]{:T(128)} %get-tuple-element.2), channel_id=1, replica_groups=mesh['rows'=32,'mask'=8] {'rows','mask'}, use_global_device_ids=true, to_apply=%region_2.3 | all-reduce | flops 1 | bytes 8 | tf_op jit(solution)/shard_map/psum | solution.py:147
  984.9 2.7 convert_element_type.293
  (24 shorter events, 1.0 us)
Async XLA Ops:
  7.2 101.0 %all-gather.2.cloned.1.call-start = ((), (), s32[]{:S(2)}) async-start(), calls=%async_computation.3 | async-start | bytes 9437184 | tf_op jit(solution)/shard_map/all_gather | solution.py:105
  8.6 109.4 %copy-start.3 = (s32[256]{0:T(256)}, s32[256]{0:T(256)S(1)}, u32[]{:S(2)}) copy-start(s32[256]{0:T(256)S(1)} %add_multiply_fusion) | copy-start | bytes 3076
  9.0 108.9 %copy-start.1 = (s32[8192]{0:T(1024)}, s32[8192]{0:T(1024)S(1)}, u32[]{:S(2)}) copy-start(s32[8192]{0:T(1024)S(1)} %iota_multiply_fusion) | copy-start | bytes 98308
  180.1 159.3 %all-to-all-start = ((bf16[2,256,8192]{1,0,2:T(2,128)(2,1)}), bf16[2,256,8192]{1,0,2:T(2,128)(2,1)}, u32[]{:S(2)}, u32[]{:S(2)}) async-start(bf16[2,256,8192]{1,0,2:T(2,128)(2,1)} %copy.72), calls=%async_computation | async-start | bytes 16777216 | tf_op jit(solution)/shard_map/all_to_all | solution.py:127
  189.6 795.3 %reduce-scatter.2.cloned.1.call-start = ((), (), s32[]{:S(2)}) async-start(), calls=%async_computation.4 | async-start | bytes 9437184 | tf_op jit(solution)/shard_map/reduce_scatter | solution.py:141
  390.4 6.6 copy-start
  724.7 21.1 %copy-start.2 = (s32[8192]{0:T(1024)S(1)}, s32[8192]{0:T(1024)}, u32[]{:S(2)}) copy-start(s32[8192]{0:T(1024)} %copy-done.1) | copy-start | bytes 98308
  724.7 21.1 %copy-start.4 = (s32[256]{0:T(256)S(1)}, s32[256]{0:T(256)}, u32[]{:S(2)}) copy-start(s32[256]{0:T(256)} %copy-done.3) | copy-start | bytes 3076
Sparse Core Ops, SparseCore 0:
  9.8 98.3 all-gather.1
  772.8 152.2 reduce-scatter.1
where the time goes:
time: 1010 us; the launch traced here: 996 us
  blocking collectives  379 us (38%)
  waiting for transfers between devices  248 us (25%)
  local copies, waits for them, and re-layouts  184 us (18%)
  other arithmetic  88.1 us (9%)
  matrix products  70.1 us (7%)
  between operations  17.2 us (2%)
    psum x1, blocking collectives, shards(): loss_total = lax.psum(loss_part, ('rows', 'mask'))  212 us
    all_to_all x1, blocking collectives, shards(): lax.all_to_all(returning, 'rows', split_axis=1, concat_axis=2, tiled=True)  168 us
    all_to_all x1, waiting for transfers between devices, shards(): lax.all_to_all(outgoing, 'rows', split_axis=2, concat_axis=1, tiled=True)  149 us
    all_gather x1, waiting for transfers between devices, shards(): slab = lax.all_gather(image_field, 'mask', axis=1, tiled=True)  98.1 us
    dot_general x8, matrix products, factor(): return jnp.einsum(form, table, values, preferred_element_type=jnp.float32)  70.1 us
    another operation x9, other arithmetic  35.3 us
    convert_element_type x2, local copies, waits for them, and re-layouts, shards(): returning = cols_inverse(weighted, inverse_tables).astype(jnp.bfloat16)  25.9 us
    convert_element_type x2, local copies, waits for them, and re-layouts, shards(): rows_forward(masked[None], forward_tables)[0].astype(jnp.bfloat16)  24.1 us
  transfers between devices with their start and end apart: 3, of which 2 were waited for; matrix products, arithmetic and copies ran while one was open for 0% of the time, Pallas kernels for 0%

commit v1 on v0

--- a/solution.py
+++ b/solution.py
@@ -102,7 +102,9 @@
 
 
 def shards(image_field, amplitudes, mask_ids):
-    slab = lax.all_gather(image_field, "mask", axis=1, tiled=True)
+    slab = jnp.concatenate(
+        lax.all_to_all(jnp.stack([image_field] * lax.axis_size("mask")), "mask", 0, 0), axis=1
+    )
     slab_rows = slab.shape[1]
     width = slab.shape[2]
     outer = width // INNER

time: 1010 us -> 1040 us (1.030)
  blocking collectives: 379 us -> 185 us
  waiting for transfers between devices: 248 us -> 409 us
  starting transfers between devices: 9.93 us -> 49.4 us
  local copies, waits for them, and re-layouts: 184 us -> 198 us
  other arithmetic: 88.1 us -> 101 us
    all_to_all x0 -> x2, waiting for transfers between devices: none -> 265 us  [the longest x1 174 us: shards(): lax.all_to_all(returning, 'rows', split_axis=1, concat_axis=2, tiled=True)]
    all_to_all x1 -> x0, blocking collectives: 168 us -> none  [shards(): lax.all_to_all(returning, 'rows', split_axis=1, concat_axis=2, tiled=True)]
    all_gather x1 -> x0, waiting for transfers between devices: 98.1 us -> none  [shards(): slab = lax.all_gather(image_field, 'mask', axis=1, tiled=True)]
    all_to_all x0 -> x2, starting transfers between devices: none -> 37.4 us  [the longest x1 31 us: shards(): lax.all_to_all(returning, 'rows', split_axis=1, concat_axis=2, tiled=True)]
    psum x1, blocking collectives: 212 us -> 185 us  [shards(): loss_total = lax.psum(loss_part, ('rows', 'mask'))]
    convert_element_type x0 -> x1, other arithmetic: none -> 11.4 us  [shards(): slab[0].astype(jnp.float32)]
    another operation x9 -> x10, other arithmetic: 35.3 us -> 46.4 us
  transfers between devices with their start and end apart: 3 -> 4, of which waited for: 2 -> 3; matrix products, arithmetic and copies ran while one was open for 0% -> 0% of each run, Pallas kernels for 0% -> 0%
where the time goes in v1:
time: 1040 us; the launch traced here: 1030 us
  waiting for transfers between devices  409 us (39%)
  local copies, waits for them, and re-layouts  198 us (19%)
  blocking collectives  185 us (18%)
  other arithmetic  101 us (10%)
  matrix products  70.2 us (7%)
  starting transfers between devices  49.4 us (5%)
  between operations  17.2 us (2%)
    psum x1, blocking collectives, shards(): loss_total = lax.psum(loss_part, ('rows', 'mask'))  185 us
    all_to_all x1, waiting for transfers between devices, shards(): lax.all_to_all(returning, 'rows', split_axis=1, concat_axis=2, tiled=True)  174 us
    all_to_all x1, waiting for transfers between devices, shards(): lax.all_to_all(outgoing, 'rows', split_axis=2, concat_axis=1, tiled=True)  143 us
    all_to_all x1, waiting for transfers between devices, shards(): lax.all_to_all(jnp.stack([image_field] * lax.axis_size('mask')), 'mask',...  90.9 us
    dot_general x8, matrix products, factor(): return jnp.einsum(form, table, values, preferred_element_type=jnp.float32)  70.2 us
    another operation x10, other arithmetic  46.4 us
    all_to_all x1, starting transfers between devices, shards(): lax.all_to_all(returning, 'rows', split_axis=1, concat_axis=2, tiled=True)  31 us
    convert_element_type x2, local copies, waits for them, and re-layouts, shards(): returning = cols_inverse(weighted, inverse_tables).astype(jnp.bfloat16)  27.8 us
  transfers between devices with their start and end apart: 4, of which 3 were waited for; matrix products, arithmetic and copies ran while one was open for 0% of the time, Pallas kernels for 0%

profile of v1, /device:TPU:1, one launch (start us, length us, event | category | flops | bytes accessed | tf_op | source)
XLA Modules:
  0.0 1029.8 jit_solution(8829209151510997980)
XLA Ops:
  7.2 5.5 stack.167
  12.7 6.4 all-to-all-start
  21.2 0.6 fusion.72
  21.9 90.9 %all-to-all-done = bf16[8,2,32,8192]{3,2,1,0:T(8,128)(2,1)} async-done(((bf16[8,2,32,8192]{3,2,1,0:T(8,128)(2,1)}), bf16[8,2,32,8192]{3,2,1,0:T(8,128)(2,1)}, u32[]{:S(2)}, u32[]{:S(2)}) %all-to-all-start) | async-done | bytes 8388640 | tf_op jit(solution)/shard_map/all_to_all | solution.py:106
  112.7 11.4 %slice_convert_fusion.1 = (f32[1,8,32,8192]{3,2,0,1:T(8,128)}, f32[1,8,32,8192]{3,2,0,1:T(8,128)}) fusion(bf16[2,8,32,8192]{3,2,0,1:T(8,128)(2,1)} %bitcast.8), kind=kLoop, calls=%fused_computation.93 | loop fusion | flops 4194304 | bytes 25165824 | tf_op jit(solution)/shard_map/convert_element_type | solution.py:125
  124.2 5.2 copy.123
  129.3 0.6 copy-done
  129.9 4.9 copy.122
  134.8 11.1 %fusion.14 = (bf16[1,256,64,128]{3,2,0,1:T(8,128)(2,1)S(1)}, bf16[1,256,64,128]{3,2,0,1:T(8,128)(2,1)}) fusion(f32[32,8,64,128]{3,2,1,0:T(8,128)S(1)} %copy.123, f32[32,8,64,128]{3,2,1,0:T(8,128)} %copy.122, s32[]{:T(128)} %bitcast.9, s32[64,128]{1,0:T(8,128)S(1)} %add_multiply_fusion, s32[256]{0:T(256)S(1)} %add_multiply_fusion.1), kind=kLoop, calls=%fused_computation.28 | loop fusion | flops 56623104 | bytes 25199620 | tf_op jit(solution)/shard_map/convert.37
  145.9 4.6 convolution_bitcast_fusion
  150.4 2.5 fusion.53
  152.9 3.7 fusion.52
  156.6 6.2 maximum_bitcast_fusion.2
  162.8 16.8 %fusion.47 = bf16[1,2,256,64,128]{2,4,1,3,0:T(8,128)(2,1)} fusion(bf16[2,256,64,128,1]{3,2,1,0,4:T(8,128)(2,1)} %maximum_bitcast_fusion.2, bf16[1,128,2,128]{3,1,2,0:T(8,128)(2,1)S(1)} %get-tuple-element.23, bf16[1,128,2,128]{3,1,2,0:T(8,128)(2,1)S(1)} %get-tuple-element.24), kind=kOutput, calls=%fused_computation.87 | convolution fusion | flops 2156134400 | bytes 16908288 | tf_op jit(solution)/shard_map/pkqj,xqraj->xprak/dot_general | solution.py:55
  179.6 7.7 copy.71
  187.3 16.4 %copy.72 = bf16[2,256,8192]{1,0,2:T(2,128)(2,1)} copy(bf16[2,256,8192]{1,2,0:T(8,128)(2,1)} %bitcast.226) | data formatting | bytes 16777216 | tf_op jit(solution)/shard_map/convert_element_type | solution.py:128
  203.7 12.0 %all-to-all-start.1 = ((bf16[2,256,8192]{1,0,2:T(2,128)(2,1)}), bf16[2,256,8192]{1,0,2:T(2,128)(2,1)}, u32[]{:S(2)}, u32[]{:S(2)}) async-start(bf16[2,256,8192]{1,0,2:T(2,128)(2,1)} %copy.72), calls=%async_computation.1 | async-start | bytes 16777216 | tf_op jit(solution)/shard_map/all_to_all | solution.py:129
  216.1 143.4 %all-to-all-done.1 = bf16[2,256,8192]{1,0,2:T(2,128)(2,1)} async-done(((bf16[2,256,8192]{1,0,2:T(2,128)(2,1)}), bf16[2,256,8192]{1,0,2:T(2,128)(2,1)}, u32[]{:S(2)}, u32[]{:S(2)}) %all-to-all-start.1) | async-done | bytes 8388640 | tf_op jit(solution)/shard_map/all_to_all | solution.py:129
  359.5 7.7 copy.73
  367.2 12.0 %copy.74 = bf16[2,32,256,256]{3,2,1,0:T(8,128)(2,1)} copy(bf16[2,32,256,256]{2,3,1,0:T(8,128)(2,1)} %bitcast.227) | data formatting | bytes 16777216 | tf_op jit(solution)/shard_map/all_to_all | solution.py:129
  379.2 9.7 fusion.42
  389.0 5.4 subtract_convert_fusion.3
  394.4 6.2 maximum_bitcast_fusion.3
  400.6 10.2 fusion.2
  410.8 6.6 fusion.101
  417.3 12.7 %fusion.6 = (f32[]{:T(128)}, bf16[1,8192,256]{2,1,0:T(8,128)(2,1)}, bf16[1,8192,256]{2,1,0:T(8,128)(2,1)}) fusion(bf16[1,8192,256]{2,1,0:T(8,128)(2,1)S(1)} %copy-done.1, f32[1,8192,256]{2,1,0:T(8,128)} %bitcast.232, f32[1,8192,256]{2,1,0:T(8,128)} %bitcast.231), kind=kLoop, calls=%fused_computation.18 | loop fusion | flops 29360128 | bytes 29360132 | tf_op jit(solution)/shard_map/reduce_sum | solution.py:137
  430.1 6.4 copy.80
  436.5 6.4 copy.79
  442.9 11.6 %convolution_bitcast_fusion.1 = f32[64,256,2,128]{3,1,2,0:T(8,128)} fusion(bf16[1,64,128,256]{2,3,0,1:T(8,128)(2,1)} %copy.80, bf16[1,64,128,256]{2,3,0,1:T(8,128)(2,1)} %copy.79, bf16[1,128,2,128]{3,1,2,0:T(8,128)(2,1)S(1)} %get-tuple-element.22, bf16[1,128,2,128]{3,1,2,0:T(8,128)(2,1)S(1)} %get-tuple-element.21), kind=kOutput, calls=%fused_computation.15 | convolution fusion | flops 2164523008 | bytes 25296896 | tf_op jit(solution)/shard_map/pkqj,qajw->pakw/dot_general | solution.py:55
  454.5 17.4 %copy.81 = f32[64,256,2,128]{1,0,3,2:T(8,128)} copy(f32[64,256,2,128]{3,1,2,0:T(8,128)} %convolution_bitcast_fusion.1) | data formatting | bytes 33554432 | tf_op jit(solution)/shard_map/pkqj,qajw->pakw/dot_general | solution.py:55
  471.9 7.9 subtract_convert_fusion.2
  479.9 4.9 fusion.1
  484.7 11.4 %copy.84 = bf16[2,64,128,256]{3,2,1,0:T(8,128)(2,1)} copy(bf16[2,64,128,256]{3,1,2,0:T(8,128)(2,1)} %fusion.1) | data formatting | bytes 16777216 | tf_op jit(solution)/shard_map/convert_element_type | solution.py:139
  496.2 16.4 %copy.85 = bf16[2,8192,256]{2,0,1:T(2,128)(2,1)} copy(bf16[2,8192,256]{2,1,0:T(8,128)(2,1)} %bitcast.228) | data formatting | bytes 16777216 | tf_op jit(solution)/shard_map/convert_element_type | solution.py:139
  512.5 31.0 %all-to-all-start.2 = ((bf16[2,8192,256]{2,0,1:T(2,128)(2,1)}), bf16[2,8192,256]{2,0,1:T(2,128)(2,1)}, u32[]{:S(2)}, u32[]{:S(2)}) async-start(bf16[2,8192,256]{2,0,1:T(2,128)(2,1)} %copy.85), calls=%async_computation.2 | async-start | bytes 16777216 | tf_op jit(solution)/shard_map/all_to_all | solution.py:140
  543.6 174.4 %all-to-all-done.2 = bf16[2,8192,256]{2,0,1:T(2,128)(2,1)} async-done(((bf16[2,8192,256]{2,0,1:T(2,128)(2,1)}), bf16[2,8192,256]{2,0,1:T(2,128)(2,1)}, u32[]{:S(2)}, u32[]{:S(2)}) %all-to-all-start.2) | async-done | bytes 8388640 | tf_op jit(solution)/shard_map/all_to_all | solution.py:140
  718.0 7.7 copy.86
  725.7 12.3 %copy.87 = bf16[2,256,32,256]{1,3,2,0:T(8,128)(2,1)} copy(bf16[2,256,32,256]{3,1,2,0:T(8,128)(2,1)} %bitcast.229) | data formatting | bytes 16777216 | tf_op jit(solution)/shard_map/all_to_all | solution.py:140
  737.9 12.0 %copy.105 = bf16[2,256,64,128,1]{3,2,0,1,4:T(8,128)(2,1)} copy(bf16[2,256,64,128,1]{1,3,2,0,4:T(8,128)(2,1)} %bitcast.230) | data formatting | bytes 16777216 | tf_op jit(solution)/shard_map/reshape.25
  750.0 5.5 convolution_bitcast_fusion.2
  755.5 2.5 fusion.50
  758.0 7.1 fusion
  765.0 20.0 %mul.951 = f32[1,2,256,8192]{3,1,2,0:T(2,128)} reshape(f32[1,2,256,64,128]{4,3,1,2,0:T(8,128)} %fusion) | data formatting | bytes 33554432 | tf_op jit(solution)/shard_map/mul | solution.py:81
  785.1 20.9 %fusion.100 = (f32[1,1,256,8192]{3,1,2,0:T(1,128)S(1)}, f32[1,1,256,8192]{3,1,2,0:T(1,128)}) fusion(f32[1,2,256,8192]{3,1,2,0:T(2,128)} %mul.951), kind=kLoop, calls=%fused_computation.173 | loop fusion | bytes 33554432 | tf_op jit(solution)/shard_map/slice | solution.py:142
  806.0 20.7 %subtract_convert_fusion = (bf16[1,256,8192]{2,1,0:T(8,128)(2,1)S(1)}, bf16[1,256,8192]{2,1,0:T(8,128)(2,1)}) fusion(f32[1,1,256,8192]{3,1,2,0:T(1,128)} %get-tuple-element.16, f32[1,1,256,8192]{3,1,2,0:T(1,128)S(1)} %get-tuple-element.15, s32[]{:T(128)} %bitcast.9, s32[8192]{0:T(1024)S(1)} %iota_multiply_fusion, s32[256]{0:T(256)S(1)} %copy-done.5), kind=kLoop, calls=%fused_computation.63 | loop fusion | flops 58720256 | bytes 25199620 | tf_op jit(solution)/shard_map/convert.3
  826.7 6.2 pad_maximum_fusion.1
  833.0 185.0 %psum.7 = f32[]{:T(128)} all-reduce(f32[]{:T(128)} %get-tuple-element.2), channel_id=1, replica_groups=mesh['rows'=32,'mask'=8] {'rows','mask'}, use_global_device_ids=true, to_apply=%region_2.3 | all-reduce | flops 1 | bytes 8 | tf_op jit(solution)/shard_map/psum | solution.py:149
  1018.6 2.7 convert_element_type.363
  (29 shorter events, 2.0 us)
Async XLA Ops:
  12.7 100.0 %all-to-all-start = ((bf16[8,2,32,8192]{3,2,1,0:T(8,128)(2,1)}), bf16[8,2,32,8192]{3,2,1,0:T(8,128)(2,1)}, u32[]{:S(2)}, u32[]{:S(2)}) async-start(bf16[8,2,32,8192]{3,2,1,0:T(8,128)(2,1)} %stack.167), calls=%async_computation | async-start | bytes 16777216 | tf_op jit(solution)/shard_map/all_to_all | solution.py:106
  19.7 115.1 %copy-start.4 = (s32[256]{0:T(256)}, s32[256]{0:T(256)S(1)}, u32[]{:S(2)}) copy-start(s32[256]{0:T(256)S(1)} %add_multiply_fusion.1) | copy-start | bytes 3076
  124.2 5.8 copy-start
  203.7 155.8 %all-to-all-start.1 = ((bf16[2,256,8192]{1,0,2:T(2,128)(2,1)}), bf16[2,256,8192]{1,0,2:T(2,128)(2,1)}, u32[]{:S(2)}, u32[]{:S(2)}) async-start(bf16[2,256,8192]{1,0,2:T(2,128)(2,1)} %copy.72), calls=%async_computation.1 | async-start | bytes 16777216 | tf_op jit(solution)/shard_map/all_to_all | solution.py:129
  410.8 6.6 copy-start.1
  471.9 7.9 copy-start.2
  471.9 7.9 copy-start.3
  512.5 205.5 %all-to-all-start.2 = ((bf16[2,8192,256]{2,0,1:T(2,128)(2,1)}), bf16[2,8192,256]{2,0,1:T(2,128)(2,1)}, u32[]{:S(2)}, u32[]{:S(2)}) async-start(bf16[2,8192,256]{2,0,1:T(2,128)(2,1)} %copy.85), calls=%async_computation.2 | async-start | bytes 16777216 | tf_op jit(solution)/shard_map/all_to_all | solution.py:140
  543.5 475.1 %reduce-scatter.2.cloned.1.call-start = ((), (), s32[]{:S(2)}) async-start(), calls=%async_computation.4 | async-start | bytes 9437184 | tf_op jit(solution)/shard_map/reduce_scatter | solution.py:143
  785.1 21.0 %copy-start.5 = (s32[256]{0:T(256)S(1)}, s32[256]{0:T(256)}, u32[]{:S(2)}) copy-start(s32[256]{0:T(256)} %copy-done.4) | copy-start | bytes 3076
Sparse Core Ops, SparseCore 0:
  833.1 123.2 reduce-scatter.1
